TPU v7x, 32 devices: a whole 2x2x4 slice. The times are simulated.
32 devices in a mesh: tm: 16 (over z, y, x), atom: 2 (over core).
Axes of the slice: x: 2, y: 2, z: 4, core: 2. Of those that a mesh axis runs over, the one named last changes fastest.
Arguments:
- positions: int32 [3, 512, 512], P(None, 'tm', 'atom'), may hold values from 0 to 16383, as said below
- velocities: float32 [3, 512, 512], P(None, 'tm', 'atom'), may hold values from -6 to 6
- species: int32 [512], P('atom'), may hold values 0 or 1
- wave_vectors: int32 [3, 256], replicated, may hold values from -64 to 64
Outputs:
- isf: float32 [6, 256, 256], P(None, 'tm', 'atom')
Inputs may be any that keep to these rules, and one draw needn't show every extreme that they name: `positions`: coordinates are fixed-point fractions of the periodic box in units of 1/16384.
All inputs are finite; a program needn't handle non-finite values. No bound on the sum of `species` on one device may be relied on, other than what follows from the above.
Results may differ from a plain program's by a relative error of at most 0.0003.
Values sent between devices are 32-bit elements; how exact they have to be, the bound alone decides.
A program may use at most 64 MiB of HBM per device.

v0:
```python
import math
import jax
import jax.numpy as jnp
from jax import lax
from jax.sharding import PartitionSpec as P

WAVE_MAX = 64
highest = lax.Precision.HIGHEST


def frame_block(pos_block, vel_block, species_onehot, wave_vectors):
    summed = (
        pos_block[0][:, :, None] * wave_vectors[0]
        + pos_block[1][:, :, None] * wave_vectors[1]
        + pos_block[2][:, :, None] * wave_vectors[2]
    )
    angle_unit = jnp.float32(2.0 * math.pi / 16384.0)
    phase = jnp.remainder(summed, 16384).astype(jnp.float32) * angle_unit
    kinds = jnp.concatenate([jnp.ones_like(vel_block[:1]), vel_block], 0)
    weights = kinds[:, None] * species_onehot[None, :, None, :]
    cos_part = jnp.einsum("qsba,bak->qsbk", weights, jnp.cos(phase), precision=highest)
    sin_part = jnp.einsum("qsba,bak->qsbk", weights, jnp.sin(phase), precision=highest)
    return jnp.stack([cos_part, sin_part])


def pair_terms(cos_rows, sin_rows):
    cos_a = cos_rows[:, :, 0]
    cos_b = cos_rows[:, :, 1]
    sin_a = sin_rows[:, :, 0]
    sin_b = sin_rows[:, :, 1]
    real_part = jnp.stack(
        [
            cos_a * cos_a + sin_a * sin_a,
            cos_a * cos_b + sin_a * sin_b,
            cos_b * cos_b + sin_b * sin_b,
        ],
        2,
    ).sum(0)
    imag_part = jnp.stack(
        [
            cos_a * sin_a - sin_a * cos_a,
            cos_a * sin_b - sin_a * cos_b,
            cos_b * sin_b - sin_b * cos_b,
        ],
        2,
    ).sum(0)
    return (real_part, imag_part)


def correlate(signals, atom_total):
    frame_total = signals.shape[-1]
    waves_here = signals.shape[3]
    signal_rows = signals.reshape(-1, frame_total)
    groups = lax.axis_size("atom")
    freq_count = frame_total // groups
    lag_count = frame_total // 2 // groups
    my_index = lax.axis_index("atom")
    freq_index = my_index * freq_count + jnp.arange(freq_count, dtype=jnp.int32)
    time_index = jnp.arange(frame_total, dtype=jnp.int32)
    angle_step = jnp.float32(math.pi / frame_total)
    turns = jnp.remainder(time_index[:, None] * freq_index[None, :], 2 * frame_total)
    angles = turns.astype(jnp.float32) * angle_step
    spec_cos = jnp.dot(signal_rows, jnp.cos(angles), precision=highest).reshape(
        2, 2, 2, waves_here, freq_count
    )
    spec_sin = jnp.dot(signal_rows, jnp.sin(angles), precision=highest).reshape(
        2, 2, 2, waves_here, freq_count
    )
    real_part, imag_part = pair_terms(spec_cos, spec_sin)
    spectral_weight = jnp.where(freq_index == 0, 1.0, 2.0).astype(jnp.float32)
    real_rows = (real_part * spectral_weight).reshape(6 * waves_here, freq_count)
    imag_rows = (imag_part * spectral_weight).reshape(6 * waves_here, freq_count)
    alternating = jnp.where(time_index % 2 == 0, 1.0, -1.0).astype(jnp.float32)
    nyquist = jnp.dot(signal_rows, alternating, precision=highest).reshape(2, 2, 2, waves_here)
    nyq_a = nyquist[:, :, 0]
    nyq_b = nyquist[:, :, 1]
    nyq_real = (
        jnp.stack([nyq_a * nyq_a, nyq_a * nyq_b, nyq_b * nyq_b], 2).sum(0).reshape(6 * waves_here)
    )
    nyq_here = nyq_real * jnp.where(my_index == 0, 1.0, 0.0).astype(jnp.float32)
    lag_index = jnp.arange(lag_count * lax.axis_size("atom"), dtype=jnp.int32)
    lag_turns = jnp.remainder(lag_index[:, None] * freq_index[None, :], 2 * frame_total)
    lag_angles = lag_turns.astype(jnp.float32) * angle_step
    term = jnp.dot(jnp.cos(lag_angles), real_rows.T, precision=highest) - jnp.dot(
        jnp.sin(lag_angles), imag_rows.T, precision=highest
    )
    lag_sign = jnp.where(lag_index % 2 == 0, 1.0, -1.0).astype(jnp.float32)
    shared = lax.psum_scatter(
        term + lag_sign[:, None] * nyq_here[None, :], "atom", scatter_dimension=0, tiled=True
    )
    lag_index = my_index * lag_count + jnp.arange(lag_count, dtype=jnp.int32)
    scaled = shared / jnp.float32(2 * frame_total)
    isf = (
        scaled / (jnp.float32(atom_total) * (frame_total - lag_index).astype(jnp.float32))[:, None]
    )
    return isf.T.reshape(6, waves_here, lag_count)


def per_device(positions, velocities, species, wave_vectors):
    atom_count = positions.shape[2]
    frame_count = positions.shape[1]
    wave_count = wave_vectors.shape[1]
    block_size = math.gcd(frame_count, 2)
    block_count = frame_count // block_size
    species_onehot = jnp.stack([1 - species, species]).astype(jnp.float32)
    pos_blocks = positions.reshape(3, block_count, block_size, atom_count).transpose(1, 0, 2, 3)
    vel_blocks = velocities.reshape(3, block_count, block_size, atom_count).transpose(1, 0, 2, 3)
    raw_modes = lax.map(
        lambda operands: frame_block(operands[0], operands[1], species_onehot, wave_vectors),
        (pos_blocks, vel_blocks),
    )
    raw_modes = raw_modes.transpose(1, 2, 3, 0, 4, 5).reshape(2, 4, 2, frame_count, wave_count)
    wave_scaled = wave_vectors.astype(jnp.float32) / WAVE_MAX
    current = (
        wave_scaled[0] * raw_modes[:, 1]
        + wave_scaled[1] * raw_modes[:, 2]
        + wave_scaled[2] * raw_modes[:, 3]
    )
    modes = jnp.stack([raw_modes[:, 0], current], 1)
    atom_groups = lax.axis_size("atom")
    summed = lax.psum(modes, "atom")
    owned = lax.all_to_all(summed, "tm", split_axis=4, concat_axis=3, tiled=True)
    signals = jnp.moveaxis(owned, 3, 4)
    return correlate(signals, atom_count * atom_groups)


def solution(mesh):
    return jax.shard_map(
        per_device,
        mesh=mesh,
        in_specs=(P(None, "tm", "atom"), P(None, "tm", "atom"), P("atom"), P()),
        out_specs=P(None, "tm", "atom"),
        check_vma=False,
    )
```

profile of v0, /device:TPU:0, one launch (start us, length us, event | category | flops | bytes accessed | tf_op | source)
XLA Modules:
  0.0 160.4 jit_solution(9982431130612515028)
XLA Ops:
  6.5 0.7 convert_multiply_fusion
  7.2 1.0 copy.23
  8.3 0.1 reshape.79
  8.3 0.6 copy-done.2
  8.9 0.7 copy-done.1
  9.6 81.0 %while.12 = (s32[]{:T(128)}, f32[16,2,4,2,2,256]{5,2,3,4,1,0:T(4,128)S(1)}, s32[16,3,2,256]{3,2,0,1:T(2,128)S(1)}, s32[3,256]{1,0:T(4,128)S(1)}, f32[16,3,2,256]...) while((s32[]{:T(128)}, f32[16,2,4,2,2,256]{5,2,3,4,1,0:T(4,128)S(1)}, ...), condition=%wide.region_1.2_spmd, body=%wide.region_0.1_spmd.sunk | while | flops 29900800 | bytes 194661 | solution.py:108
  9.7 2.5 %convolution_bitcast_fusion.5 = f32[1,4,2,2,256]{4,1,2,3,0:T(4,128)S(1)} fusion(s32[256]{0:T(256)S(1)} %bitcast.119, s32[2,256]{1,0:T(2,128)S(1)} %get-tuple-element.188, s32[256]{0:T(256)S(1)} %bitcast.121, s32[2,256]{1,0:T(2,128)S(1)} %get-tuple-element.190, s32[256]{0:T(256)S(1)} %bitcast.117, s32[2,256]{1,0:T(2,128)S(1)} %get-tuple-element.192, ...), kind=kOutput, calls=%fused_computation.1.clone.1 | convolution fusion | flops 14946304 | bytes 35840 | tf_op jit(solution)/shard_map/while/body/eval_jaxpr/qsba,bak->qsbk/dot_general | solution.py:21
  12.1 2.5 %convolution_bitcast_fusion.4 = f32[1,4,2,2,256]{4,1,2,3,0:T(4,128)S(1)} fusion(s32[256]{0:T(256)S(1)} %bitcast.120, s32[2,256]{1,0:T(2,128)S(1)} %get-tuple-element.188, s32[256]{0:T(256)S(1)} %bitcast.122, s32[2,256]{1,0:T(2,128)S(1)} %get-tuple-element.190, s32[256]{0:T(256)S(1)} %bitcast.118, s32[2,256]{1,0:T(2,128)S(1)} %get-tuple-element.192, ...), kind=kOutput, calls=%fused_computation.clone.1 | convolution fusion | flops 14946304 | bytes 35840 | tf_op jit(solution)/shard_map/while/body/eval_jaxpr/qsba,bak->qsbk/dot_general | solution.py:22
  14.7 2.5 %convolution_bitcast_fusion.5 = f32[1,4,2,2,256]{4,1,2,3,0:T(4,128)S(1)} fusion(s32[256]{0:T(256)S(1)} %bitcast.119, s32[2,256]{1,0:T(2,128)S(1)} %get-tuple-element.188, s32[256]{0:T(256)S(1)} %bitcast.121, s32[2,256]{1,0:T(2,128)S(1)} %get-tuple-element.190, s32[256]{0:T(256)S(1)} %bitcast.117, s32[2,256]{1,0:T(2,128)S(1)} %get-tuple-element.192, ...), kind=kOutput, calls=%fused_computation.1.clone.1 | convolution fusion | flops 14946304 | bytes 35840 | tf_op jit(solution)/shard_map/while/body/eval_jaxpr/qsba,bak->qsbk/dot_general | solution.py:21
  17.2 2.5 %convolution_bitcast_fusion.4 = f32[1,4,2,2,256]{4,1,2,3,0:T(4,128)S(1)} fusion(s32[256]{0:T(256)S(1)} %bitcast.120, s32[2,256]{1,0:T(2,128)S(1)} %get-tuple-element.188, s32[256]{0:T(256)S(1)} %bitcast.122, s32[2,256]{1,0:T(2,128)S(1)} %get-tuple-element.190, s32[256]{0:T(256)S(1)} %bitcast.118, s32[2,256]{1,0:T(2,128)S(1)} %get-tuple-element.192, ...), kind=kOutput, calls=%fused_computation.clone.1 | convolution fusion | flops 14946304 | bytes 35840 | tf_op jit(solution)/shard_map/while/body/eval_jaxpr/qsba,bak->qsbk/dot_general | solution.py:22
  19.8 2.5 %convolution_bitcast_fusion.5 = f32[1,4,2,2,256]{4,1,2,3,0:T(4,128)S(1)} fusion(s32[256]{0:T(256)S(1)} %bitcast.119, s32[2,256]{1,0:T(2,128)S(1)} %get-tuple-element.188, s32[256]{0:T(256)S(1)} %bitcast.121, s32[2,256]{1,0:T(2,128)S(1)} %get-tuple-element.190, s32[256]{0:T(256)S(1)} %bitcast.117, s32[2,256]{1,0:T(2,128)S(1)} %get-tuple-element.192, ...), kind=kOutput, calls=%fused_computation.1.clone.1 | convolution fusion | flops 14946304 | bytes 35840 | tf_op jit(solution)/shard_map/while/body/eval_jaxpr/qsba,bak->qsbk/dot_general | solution.py:21
  22.2 2.5 %convolution_bitcast_fusion.4 = f32[1,4,2,2,256]{4,1,2,3,0:T(4,128)S(1)} fusion(s32[256]{0:T(256)S(1)} %bitcast.120, s32[2,256]{1,0:T(2,128)S(1)} %get-tuple-element.188, s32[256]{0:T(256)S(1)} %bitcast.122, s32[2,256]{1,0:T(2,128)S(1)} %get-tuple-element.190, s32[256]{0:T(256)S(1)} %bitcast.118, s32[2,256]{1,0:T(2,128)S(1)} %get-tuple-element.192, ...), kind=kOutput, calls=%fused_computation.clone.1 | convolution fusion | flops 14946304 | bytes 35840 | tf_op jit(solution)/shard_map/while/body/eval_jaxpr/qsba,bak->qsbk/dot_general | solution.py:22
  24.9 2.5 %convolution_bitcast_fusion.5 = f32[1,4,2,2,256]{4,1,2,3,0:T(4,128)S(1)} fusion(s32[256]{0:T(256)S(1)} %bitcast.119, s32[2,256]{1,0:T(2,128)S(1)} %get-tuple-element.188, s32[256]{0:T(256)S(1)} %bitcast.121, s32[2,256]{1,0:T(2,128)S(1)} %get-tuple-element.190, s32[256]{0:T(256)S(1)} %bitcast.117, s32[2,256]{1,0:T(2,128)S(1)} %get-tuple-element.192, ...), kind=kOutput, calls=%fused_computation.1.clone.1 | convolution fusion | flops 14946304 | bytes 35840 | tf_op jit(solution)/shard_map/while/body/eval_jaxpr/qsba,bak->qsbk/dot_general | solution.py:21
  27.3 2.5 %convolution_bitcast_fusion.4 = f32[1,4,2,2,256]{4,1,2,3,0:T(4,128)S(1)} fusion(s32[256]{0:T(256)S(1)} %bitcast.120, s32[2,256]{1,0:T(2,128)S(1)} %get-tuple-element.188, s32[256]{0:T(256)S(1)} %bitcast.122, s32[2,256]{1,0:T(2,128)S(1)} %get-tuple-element.190, s32[256]{0:T(256)S(1)} %bitcast.118, s32[2,256]{1,0:T(2,128)S(1)} %get-tuple-element.192, ...), kind=kOutput, calls=%fused_computation.clone.1 | convolution fusion | flops 14946304 | bytes 35840 | tf_op jit(solution)/shard_map/while/body/eval_jaxpr/qsba,bak->qsbk/dot_general | solution.py:22
  29.9 2.5 %convolution_bitcast_fusion.5 = f32[1,4,2,2,256]{4,1,2,3,0:T(4,128)S(1)} fusion(s32[256]{0:T(256)S(1)} %bitcast.119, s32[2,256]{1,0:T(2,128)S(1)} %get-tuple-element.188, s32[256]{0:T(256)S(1)} %bitcast.121, s32[2,256]{1,0:T(2,128)S(1)} %get-tuple-element.190, s32[256]{0:T(256)S(1)} %bitcast.117, s32[2,256]{1,0:T(2,128)S(1)} %get-tuple-element.192, ...), kind=kOutput, calls=%fused_computation.1.clone.1 | convolution fusion | flops 14946304 | bytes 35840 | tf_op jit(solution)/shard_map/while/body/eval_jaxpr/qsba,bak->qsbk/dot_general | solution.py:21
  32.4 2.5 %convolution_bitcast_fusion.4 = f32[1,4,2,2,256]{4,1,2,3,0:T(4,128)S(1)} fusion(s32[256]{0:T(256)S(1)} %bitcast.120, s32[2,256]{1,0:T(2,128)S(1)} %get-tuple-element.188, s32[256]{0:T(256)S(1)} %bitcast.122, s32[2,256]{1,0:T(2,128)S(1)} %get-tuple-element.190, s32[256]{0:T(256)S(1)} %bitcast.118, s32[2,256]{1,0:T(2,128)S(1)} %get-tuple-element.192, ...), kind=kOutput, calls=%fused_computation.clone.1 | convolution fusion | flops 14946304 | bytes 35840 | tf_op jit(solution)/shard_map/while/body/eval_jaxpr/qsba,bak->qsbk/dot_general | solution.py:22
  35.0 2.5 %convolution_bitcast_fusion.5 = f32[1,4,2,2,256]{4,1,2,3,0:T(4,128)S(1)} fusion(s32[256]{0:T(256)S(1)} %bitcast.119, s32[2,256]{1,0:T(2,128)S(1)} %get-tuple-element.188, s32[256]{0:T(256)S(1)} %bitcast.121, s32[2,256]{1,0:T(2,128)S(1)} %get-tuple-element.190, s32[256]{0:T(256)S(1)} %bitcast.117, s32[2,256]{1,0:T(2,128)S(1)} %get-tuple-element.192, ...), kind=kOutput, calls=%fused_computation.1.clone.1 | convolution fusion | flops 14946304 | bytes 35840 | tf_op jit(solution)/shard_map/while/body/eval_jaxpr/qsba,bak->qsbk/dot_general | solution.py:21
  37.4 2.5 %convolution_bitcast_fusion.4 = f32[1,4,2,2,256]{4,1,2,3,0:T(4,128)S(1)} fusion(s32[256]{0:T(256)S(1)} %bitcast.120, s32[2,256]{1,0:T(2,128)S(1)} %get-tuple-element.188, s32[256]{0:T(256)S(1)} %bitcast.122, s32[2,256]{1,0:T(2,128)S(1)} %get-tuple-element.190, s32[256]{0:T(256)S(1)} %bitcast.118, s32[2,256]{1,0:T(2,128)S(1)} %get-tuple-element.192, ...), kind=kOutput, calls=%fused_computation.clone.1 | convolution fusion | flops 14946304 | bytes 35840 | tf_op jit(solution)/shard_map/while/body/eval_jaxpr/qsba,bak->qsbk/dot_general | solution.py:22
  40.1 2.5 %convolution_bitcast_fusion.5 = f32[1,4,2,2,256]{4,1,2,3,0:T(4,128)S(1)} fusion(s32[256]{0:T(256)S(1)} %bitcast.119, s32[2,256]{1,0:T(2,128)S(1)} %get-tuple-element.188, s32[256]{0:T(256)S(1)} %bitcast.121, s32[2,256]{1,0:T(2,128)S(1)} %get-tuple-element.190, s32[256]{0:T(256)S(1)} %bitcast.117, s32[2,256]{1,0:T(2,128)S(1)} %get-tuple-element.192, ...), kind=kOutput, calls=%fused_computation.1.clone.1 | convolution fusion | flops 14946304 | bytes 35840 | tf_op jit(solution)/shard_map/while/body/eval_jaxpr/qsba,bak->qsbk/dot_general | solution.py:21
  42.5 2.5 %convolution_bitcast_fusion.4 = f32[1,4,2,2,256]{4,1,2,3,0:T(4,128)S(1)} fusion(s32[256]{0:T(256)S(1)} %bitcast.120, s32[2,256]{1,0:T(2,128)S(1)} %get-tuple-element.188, s32[256]{0:T(256)S(1)} %bitcast.122, s32[2,256]{1,0:T(2,128)S(1)} %get-tuple-element.190, s32[256]{0:T(256)S(1)} %bitcast.118, s32[2,256]{1,0:T(2,128)S(1)} %get-tuple-element.192, ...), kind=kOutput, calls=%fused_computation.clone.1 | convolution fusion | flops 14946304 | bytes 35840 | tf_op jit(solution)/shard_map/while/body/eval_jaxpr/qsba,bak->qsbk/dot_general | solution.py:22
  45.1 2.5 %convolution_bitcast_fusion.5 = f32[1,4,2,2,256]{4,1,2,3,0:T(4,128)S(1)} fusion(s32[256]{0:T(256)S(1)} %bitcast.119, s32[2,256]{1,0:T(2,128)S(1)} %get-tuple-element.188, s32[256]{0:T(256)S(1)} %bitcast.121, s32[2,256]{1,0:T(2,128)S(1)} %get-tuple-element.190, s32[256]{0:T(256)S(1)} %bitcast.117, s32[2,256]{1,0:T(2,128)S(1)} %get-tuple-element.192, ...), kind=kOutput, calls=%fused_computation.1.clone.1 | convolution fusion | flops 14946304 | bytes 35840 | tf_op jit(solution)/shard_map/while/body/eval_jaxpr/qsba,bak->qsbk/dot_general | solution.py:21
  47.6 2.5 %convolution_bitcast_fusion.4 = f32[1,4,2,2,256]{4,1,2,3,0:T(4,128)S(1)} fusion(s32[256]{0:T(256)S(1)} %bitcast.120, s32[2,256]{1,0:T(2,128)S(1)} %get-tuple-element.188, s32[256]{0:T(256)S(1)} %bitcast.122, s32[2,256]{1,0:T(2,128)S(1)} %get-tuple-element.190, s32[256]{0:T(256)S(1)} %bitcast.118, s32[2,256]{1,0:T(2,128)S(1)} %get-tuple-element.192, ...), kind=kOutput, calls=%fused_computation.clone.1 | convolution fusion | flops 14946304 | bytes 35840 | tf_op jit(solution)/shard_map/while/body/eval_jaxpr/qsba,bak->qsbk/dot_general | solution.py:22
  50.2 2.5 %convolution_bitcast_fusion.5 = f32[1,4,2,2,256]{4,1,2,3,0:T(4,128)S(1)} fusion(s32[256]{0:T(256)S(1)} %bitcast.119, s32[2,256]{1,0:T(2,128)S(1)} %get-tuple-element.188, s32[256]{0:T(256)S(1)} %bitcast.121, s32[2,256]{1,0:T(2,128)S(1)} %get-tuple-element.190, s32[256]{0:T(256)S(1)} %bitcast.117, s32[2,256]{1,0:T(2,128)S(1)} %get-tuple-element.192, ...), kind=kOutput, calls=%fused_computation.1.clone.1 | convolution fusion | flops 14946304 | bytes 35840 | tf_op jit(solution)/shard_map/while/body/eval_jaxpr/qsba,bak->qsbk/dot_general | solution.py:21
  52.6 2.5 %convolution_bitcast_fusion.4 = f32[1,4,2,2,256]{4,1,2,3,0:T(4,128)S(1)} fusion(s32[256]{0:T(256)S(1)} %bitcast.120, s32[2,256]{1,0:T(2,128)S(1)} %get-tuple-element.188, s32[256]{0:T(256)S(1)} %bitcast.122, s32[2,256]{1,0:T(2,128)S(1)} %get-tuple-element.190, s32[256]{0:T(256)S(1)} %bitcast.118, s32[2,256]{1,0:T(2,128)S(1)} %get-tuple-element.192, ...), kind=kOutput, calls=%fused_computation.clone.1 | convolution fusion | flops 14946304 | bytes 35840 | tf_op jit(solution)/shard_map/while/body/eval_jaxpr/qsba,bak->qsbk/dot_general | solution.py:22
  55.3 2.5 %convolution_bitcast_fusion.5 = f32[1,4,2,2,256]{4,1,2,3,0:T(4,128)S(1)} fusion(s32[256]{0:T(256)S(1)} %bitcast.119, s32[2,256]{1,0:T(2,128)S(1)} %get-tuple-element.188, s32[256]{0:T(256)S(1)} %bitcast.121, s32[2,256]{1,0:T(2,128)S(1)} %get-tuple-element.190, s32[256]{0:T(256)S(1)} %bitcast.117, s32[2,256]{1,0:T(2,128)S(1)} %get-tuple-element.192, ...), kind=kOutput, calls=%fused_computation.1.clone.1 | convolution fusion | flops 14946304 | bytes 35840 | tf_op jit(solution)/shard_map/while/body/eval_jaxpr/qsba,bak->qsbk/dot_general | solution.py:21
  57.7 2.5 %convolution_bitcast_fusion.4 = f32[1,4,2,2,256]{4,1,2,3,0:T(4,128)S(1)} fusion(s32[256]{0:T(256)S(1)} %bitcast.120, s32[2,256]{1,0:T(2,128)S(1)} %get-tuple-element.188, s32[256]{0:T(256)S(1)} %bitcast.122, s32[2,256]{1,0:T(2,128)S(1)} %get-tuple-element.190, s32[256]{0:T(256)S(1)} %bitcast.118, s32[2,256]{1,0:T(2,128)S(1)} %get-tuple-element.192, ...), kind=kOutput, calls=%fused_computation.clone.1 | convolution fusion | flops 14946304 | bytes 35840 | tf_op jit(solution)/shard_map/while/body/eval_jaxpr/qsba,bak->qsbk/dot_general | solution.py:22
  60.3 2.5 %convolution_bitcast_fusion.5 = f32[1,4,2,2,256]{4,1,2,3,0:T(4,128)S(1)} fusion(s32[256]{0:T(256)S(1)} %bitcast.119, s32[2,256]{1,0:T(2,128)S(1)} %get-tuple-element.188, s32[256]{0:T(256)S(1)} %bitcast.121, s32[2,256]{1,0:T(2,128)S(1)} %get-tuple-element.190, s32[256]{0:T(256)S(1)} %bitcast.117, s32[2,256]{1,0:T(2,128)S(1)} %get-tuple-element.192, ...), kind=kOutput, calls=%fused_computation.1.clone.1 | convolution fusion | flops 14946304 | bytes 35840 | tf_op jit(solution)/shard_map/while/body/eval_jaxpr/qsba,bak->qsbk/dot_general | solution.py:21
  62.8 2.5 %convolution_bitcast_fusion.4 = f32[1,4,2,2,256]{4,1,2,3,0:T(4,128)S(1)} fusion(s32[256]{0:T(256)S(1)} %bitcast.120, s32[2,256]{1,0:T(2,128)S(1)} %get-tuple-element.188, s32[256]{0:T(256)S(1)} %bitcast.122, s32[2,256]{1,0:T(2,128)S(1)} %get-tuple-element.190, s32[256]{0:T(256)S(1)} %bitcast.118, s32[2,256]{1,0:T(2,128)S(1)} %get-tuple-element.192, ...), kind=kOutput, calls=%fused_computation.clone.1 | convolution fusion | flops 14946304 | bytes 35840 | tf_op jit(solution)/shard_map/while/body/eval_jaxpr/qsba,bak->qsbk/dot_general | solution.py:22
  65.4 2.5 %convolution_bitcast_fusion.5 = f32[1,4,2,2,256]{4,1,2,3,0:T(4,128)S(1)} fusion(s32[256]{0:T(256)S(1)} %bitcast.119, s32[2,256]{1,0:T(2,128)S(1)} %get-tuple-element.188, s32[256]{0:T(256)S(1)} %bitcast.121, s32[2,256]{1,0:T(2,128)S(1)} %get-tuple-element.190, s32[256]{0:T(256)S(1)} %bitcast.117, s32[2,256]{1,0:T(2,128)S(1)} %get-tuple-element.192, ...), kind=kOutput, calls=%fused_computation.1.clone.1 | convolution fusion | flops 14946304 | bytes 35840 | tf_op jit(solution)/shard_map/while/body/eval_jaxpr/qsba,bak->qsbk/dot_general | solution.py:21
  67.8 2.5 %convolution_bitcast_fusion.4 = f32[1,4,2,2,256]{4,1,2,3,0:T(4,128)S(1)} fusion(s32[256]{0:T(256)S(1)} %bitcast.120, s32[2,256]{1,0:T(2,128)S(1)} %get-tuple-element.188, s32[256]{0:T(256)S(1)} %bitcast.122, s32[2,256]{1,0:T(2,128)S(1)} %get-tuple-element.190, s32[256]{0:T(256)S(1)} %bitcast.118, s32[2,256]{1,0:T(2,128)S(1)} %get-tuple-element.192, ...), kind=kOutput, calls=%fused_computation.clone.1 | convolution fusion | flops 14946304 | bytes 35840 | tf_op jit(solution)/shard_map/while/body/eval_jaxpr/qsba,bak->qsbk/dot_general | solution.py:22
  70.5 2.5 %convolution_bitcast_fusion.5 = f32[1,4,2,2,256]{4,1,2,3,0:T(4,128)S(1)} fusion(s32[256]{0:T(256)S(1)} %bitcast.119, s32[2,256]{1,0:T(2,128)S(1)} %get-tuple-element.188, s32[256]{0:T(256)S(1)} %bitcast.121, s32[2,256]{1,0:T(2,128)S(1)} %get-tuple-element.190, s32[256]{0:T(256)S(1)} %bitcast.117, s32[2,256]{1,0:T(2,128)S(1)} %get-tuple-element.192, ...), kind=kOutput, calls=%fused_computation.1.clone.1 | convolution fusion | flops 14946304 | bytes 35840 | tf_op jit(solution)/shard_map/while/body/eval_jaxpr/qsba,bak->qsbk/dot_general | solution.py:21
  72.9 2.5 %convolution_bitcast_fusion.4 = f32[1,4,2,2,256]{4,1,2,3,0:T(4,128)S(1)} fusion(s32[256]{0:T(256)S(1)} %bitcast.120, s32[2,256]{1,0:T(2,128)S(1)} %get-tuple-element.188, s32[256]{0:T(256)S(1)} %bitcast.122, s32[2,256]{1,0:T(2,128)S(1)} %get-tuple-element.190, s32[256]{0:T(256)S(1)} %bitcast.118, s32[2,256]{1,0:T(2,128)S(1)} %get-tuple-element.192, ...), kind=kOutput, calls=%fused_computation.clone.1 | convolution fusion | flops 14946304 | bytes 35840 | tf_op jit(solution)/shard_map/while/body/eval_jaxpr/qsba,bak->qsbk/dot_general | solution.py:22
  75.5 2.5 %convolution_bitcast_fusion.5 = f32[1,4,2,2,256]{4,1,2,3,0:T(4,128)S(1)} fusion(s32[256]{0:T(256)S(1)} %bitcast.119, s32[2,256]{1,0:T(2,128)S(1)} %get-tuple-element.188, s32[256]{0:T(256)S(1)} %bitcast.121, s32[2,256]{1,0:T(2,128)S(1)} %get-tuple-element.190, s32[256]{0:T(256)S(1)} %bitcast.117, s32[2,256]{1,0:T(2,128)S(1)} %get-tuple-element.192, ...), kind=kOutput, calls=%fused_computation.1.clone.1 | convolution fusion | flops 14946304 | bytes 35840 | tf_op jit(solution)/shard_map/while/body/eval_jaxpr/qsba,bak->qsbk/dot_general | solution.py:21
  78.0 2.5 %convolution_bitcast_fusion.4 = f32[1,4,2,2,256]{4,1,2,3,0:T(4,128)S(1)} fusion(s32[256]{0:T(256)S(1)} %bitcast.120, s32[2,256]{1,0:T(2,128)S(1)} %get-tuple-element.188, s32[256]{0:T(256)S(1)} %bitcast.122, s32[2,256]{1,0:T(2,128)S(1)} %get-tuple-element.190, s32[256]{0:T(256)S(1)} %bitcast.118, s32[2,256]{1,0:T(2,128)S(1)} %get-tuple-element.192, ...), kind=kOutput, calls=%fused_computation.clone.1 | convolution fusion | flops 14946304 | bytes 35840 | tf_op jit(solution)/shard_map/while/body/eval_jaxpr/qsba,bak->qsbk/dot_general | solution.py:22
  80.6 2.5 %convolution_bitcast_fusion.5 = f32[1,4,2,2,256]{4,1,2,3,0:T(4,128)S(1)} fusion(s32[256]{0:T(256)S(1)} %bitcast.119, s32[2,256]{1,0:T(2,128)S(1)} %get-tuple-element.188, s32[256]{0:T(256)S(1)} %bitcast.121, s32[2,256]{1,0:T(2,128)S(1)} %get-tuple-element.190, s32[256]{0:T(256)S(1)} %bitcast.117, s32[2,256]{1,0:T(2,128)S(1)} %get-tuple-element.192, ...), kind=kOutput, calls=%fused_computation.1.clone.1 | convolution fusion | flops 14946304 | bytes 35840 | tf_op jit(solution)/shard_map/while/body/eval_jaxpr/qsba,bak->qsbk/dot_general | solution.py:21
  83.0 2.5 %convolution_bitcast_fusion.4 = f32[1,4,2,2,256]{4,1,2,3,0:T(4,128)S(1)} fusion(s32[256]{0:T(256)S(1)} %bitcast.120, s32[2,256]{1,0:T(2,128)S(1)} %get-tuple-element.188, s32[256]{0:T(256)S(1)} %bitcast.122, s32[2,256]{1,0:T(2,128)S(1)} %get-tuple-element.190, s32[256]{0:T(256)S(1)} %bitcast.118, s32[2,256]{1,0:T(2,128)S(1)} %get-tuple-element.192, ...), kind=kOutput, calls=%fused_computation.clone.1 | convolution fusion | flops 14946304 | bytes 35840 | tf_op jit(solution)/shard_map/while/body/eval_jaxpr/qsba,bak->qsbk/dot_general | solution.py:22
  85.7 2.5 %convolution_bitcast_fusion.5 = f32[1,4,2,2,256]{4,1,2,3,0:T(4,128)S(1)} fusion(s32[256]{0:T(256)S(1)} %bitcast.119, s32[2,256]{1,0:T(2,128)S(1)} %get-tuple-element.188, s32[256]{0:T(256)S(1)} %bitcast.121, s32[2,256]{1,0:T(2,128)S(1)} %get-tuple-element.190, s32[256]{0:T(256)S(1)} %bitcast.117, s32[2,256]{1,0:T(2,128)S(1)} %get-tuple-element.192, ...), kind=kOutput, calls=%fused_computation.1.clone.1 | convolution fusion | flops 14946304 | bytes 35840 | tf_op jit(solution)/shard_map/while/body/eval_jaxpr/qsba,bak->qsbk/dot_general | solution.py:21
  88.1 2.5 %convolution_bitcast_fusion.4 = f32[1,4,2,2,256]{4,1,2,3,0:T(4,128)S(1)} fusion(s32[256]{0:T(256)S(1)} %bitcast.120, s32[2,256]{1,0:T(2,128)S(1)} %get-tuple-element.188, s32[256]{0:T(256)S(1)} %bitcast.122, s32[2,256]{1,0:T(2,128)S(1)} %get-tuple-element.190, s32[256]{0:T(256)S(1)} %bitcast.118, s32[2,256]{1,0:T(2,128)S(1)} %get-tuple-element.192, ...), kind=kOutput, calls=%fused_computation.clone.1 | convolution fusion | flops 14946304 | bytes 35840 | tf_op jit(solution)/shard_map/while/body/eval_jaxpr/qsba,bak->qsbk/dot_general | solution.py:22
  90.6 0.3 copy.25
  90.9 0.1 fusion.78
  91.1 0.8 pad_maximum_fusion
  91.9 0.0 all-reduce.3.cloned.1.call-update
  91.9 21.1 %all-reduce.3.cloned.1.call-done = f32[2,2,2,32,256]{4,2,3,1,0:T(2,128)} async-done(((f32[2,2,2,32,256]{4,2,3,1,0:T(2,128)}), f32[2,2,2,32,256]{4,2,3,1,0:T(2,128)}) %all-reduce.3.cloned.1.call-update) | async-done | bytes 262160 | tf_op jit(solution)/shard_map/psum | solution.py:121
  113.0 1.6 %copy.26 = f32[2,2,2,32,256]{3,2,1,0,4:T(2,128)S(1)} copy(f32[2,2,2,32,256]{4,2,3,1,0:T(2,128)} %all-reduce.3.cloned.1.call-done) | data formatting | bytes 524288 | tf_op jit(solution)/shard_map/psum | solution.py:121
  114.7 1.7 %reshape.89 = f32[16,1,4096]{2,1,0:T(1,128)} reshape(f32[256,2,2,2,32]{4,3,2,1,0:T(2,128)S(1)} %bitcast.110) | data formatting | bytes 524288
  116.4 6.8 %all-to-all-start = ((f32[16,1,4096]{2,1,0:T(1,128)}), f32[16,1,4096]{2,1,0:T(1,128)S(1)}, u32[]{:S(2)}, u32[]{:S(2)}) async-start(f32[16,1,4096]{2,1,0:T(1,128)} %reshape.89), calls=%async_computation | async-start | bytes 524288 | tf_op jit(solution)/shard_map/all_to_all | solution.py:122
  123.2 0.2 reduce-scatter.2.cloned.1.call-start
  123.5 10.0 %all-to-all-done = f32[16,1,4096]{2,1,0:T(1,128)S(1)} async-done(((f32[16,1,4096]{2,1,0:T(1,128)}), f32[16,1,4096]{2,1,0:T(1,128)S(1)}, u32[]{:S(2)}, u32[]{:S(2)}) %all-to-all-start) | async-done | bytes 262176 | tf_op jit(solution)/shard_map/all_to_all | solution.py:122
  133.5 0.5 broadcast.151
  134.0 1.3 reduce
  135.3 0.9 reshape.90
  136.2 0.2 copy.27
  136.4 0.3 copy.28
  136.8 0.4 all_to_all.16
  137.2 2.3 %fusion.28 = f32[2,2,2,16,256]{4,3,2,1,0:T(8,128)S(1)} fusion(f32[2,2,2,512,16]{3,4,2,1,0:T(8,128)S(1)} %all_to_all.16, s32[256]{0:T(256)S(1)} %iota_add_fusion), kind=kOutput, calls=%fused_computation.41 | convolution fusion | flops 203161600 | bytes 394240 | tf_op jit(solution)/shard_map/dot_general | solution.py:66
  139.5 2.3 %fusion.30 = f32[2,2,2,16,256]{4,3,2,1,0:T(8,128)S(1)} fusion(f32[2,2,2,512,16]{3,4,2,1,0:T(8,128)S(1)} %all_to_all.16, s32[256]{0:T(256)S(1)} %iota_add_fusion), kind=kOutput, calls=%fused_computation.43 | convolution fusion | flops 203161600 | bytes 394240 | tf_op jit(solution)/shard_map/dot_general | solution.py:63
  141.9 0.1 multiply_subtract_fusion.2
  142.0 1.3 fusion.47
  143.3 1.0 fusion.40
  144.4 0.1 mul.346
  144.5 2.0 %fusion.24 = f32[256,96]{0,1:T(8,128)} fusion(f32[256,96]{0,1:T(8,128)S(1)} %fusion.47, f32[96,256]{1,0:T(8,128)S(1)} %get-tuple-element.140, s32[256]{0:T(256)S(1)} %iota_add_fusion, f32[96]{0:T(128)S(1)} %mul.346, f32[256]{0:T(256)S(1)} %compare_select_fusion), kind=kOutput, calls=%fused_computation.34 | convolution fusion | flops 76488704 | bytes 297344 | tf_op jit(solution)/shard_map/dot_general | solution.py:84
  146.5 0.0 reduce-scatter.2.cloned.1.call-update
  146.5 5.6 %reduce-scatter.2.cloned.1.call-done = f32[128,96]{0,1:T(8,128)} async-done(((f32[256,96]{0,1:T(8,128)}), f32[128,96]{0,1:T(8,128)}) %reduce-scatter.2.cloned.1.call-update) | async-done | bytes 49168 | tf_op jit(solution)/shard_map/reduce_scatter | solution.py:88
  152.1 1.4 multiply_divide_fusion
  (117 shorter events, 1.1 us)
Async XLA Ops:
  6.5 106.5 %all-reduce.3.cloned.1.call-start = ((), (), s32[]{:S(2)}) async-start(), calls=%async_computation.2 | async-start | bytes 524288 | tf_op jit(solution)/shard_map/psum | solution.py:121
  7.2 1.0 copy-start
  8.2 0.7 copy-start.2
  8.9 0.7 copy-start.1
  116.4 17.1 %all-to-all-start = ((f32[16,1,4096]{2,1,0:T(1,128)}), f32[16,1,4096]{2,1,0:T(1,128)S(1)}, u32[]{:S(2)}, u32[]{:S(2)}) async-start(f32[16,1,4096]{2,1,0:T(1,128)} %reshape.89), calls=%async_computation | async-start | bytes 524288 | tf_op jit(solution)/shard_map/all_to_all | solution.py:122
  123.2 28.9 %reduce-scatter.2.cloned.1.call-start = ((), (), s32[]{:S(2)}) async-start(), calls=%async_computation.3 | async-start | bytes 147456 | tf_op jit(solution)/shard_map/reduce_scatter | solution.py:88
Sparse Core Ops, SparseCore 0:
  92.0 20.9 all-reduce.2
  146.7 5.4 reduce-scatter.1
where the time goes:
time: 161 us; the launch traced here: 160 us
  matrix products  88.1 us (55%)
  waiting for transfers between devices  36.8 us (23%)
  between operations  13.6 us (8%)
  local copies, waits for them, and re-layouts  8.99 us (6%)
  starting transfers between devices  7.01 us (4%)
  other arithmetic  4.92 us (3%)
    dot_general x16, matrix products, frame_block(): jnp.einsum('qsba,bak->qsbk', weights, jnp.sin(phase), precision=highest)  39.8 us
    dot_general x16, matrix products, frame_block(): jnp.einsum('qsba,bak->qsbk', weights, jnp.cos(phase), precision=highest)  39.3 us
    psum x1, waiting for transfers between devices, per_device(): summed = lax.psum(modes, 'atom')  21.1 us
    all_to_all x1, waiting for transfers between devices, per_device(): lax.all_to_all(summed, 'tm', split_axis=4, concat_axis=3, tiled=True)  10 us
    all_to_all x1, starting transfers between devices, per_device(): lax.all_to_all(summed, 'tm', split_axis=4, concat_axis=3, tiled=True)  6.78 us
    reduce_scatter x1, waiting for transfers between devices, correlate(): lax.psum_scatter(term + lag_sign[:, None] * nyq_here[None, :], 'atom', sc...  5.55 us
    unnamed x9, local copies, waits for them, and re-layouts  4.93 us
  transfers between devices with their start and end apart: 3, of which 3 were waited for; matrix products, arithmetic and copies ran while one was open for 0% of the time, Pallas kernels for 0%

commit v1 on v0

--- a/solution.py
+++ b/solution.py
@@ -6,6 +6,13 @@
 
 WAVE_MAX = 64
 highest = lax.Precision.HIGHEST
+
+
+def swap_blocks(x, name, split, join):
+    size = lax.axis_size(name)
+    blocks = jnp.stack(jnp.split(x, size, axis=split), axis=0)
+    blocks = lax.all_to_all(blocks, name, split_axis=0, concat_axis=0)
+    return jnp.concatenate(blocks, axis=join)
 
 
 def frame_block(pos_block, vel_block, species_onehot, wave_vectors):
@@ -119,7 +126,7 @@
     modes = jnp.stack([raw_modes[:, 0], current], 1)
     atom_groups = lax.axis_size("atom")
     summed = lax.psum(modes, "atom")
-    owned = lax.all_to_all(summed, "tm", split_axis=4, concat_axis=3, tiled=True)
+    owned = swap_blocks(summed, "tm", 4, 3)
     signals = jnp.moveaxis(owned, 3, 4)
     return correlate(signals, atom_count * atom_groups)
 

time: 161 us -> 184 us (1.14)
  local copies, waits for them, and re-layouts: 8.99 us -> 30.6 us
    slice x16, local copies, waits for them, and re-layouts: 0.08 us -> 12.9 us  [frame_block(): wave_vectors[0]]
    unnamed x9 -> x20, local copies, waits for them, and re-layouts: 4.93 us -> 13.1 us
where the time goes in v1:
time: 184 us; the launch traced here: 183 us
  matrix products  88.1 us (48%)
  waiting for transfers between devices  36.7 us (20%)
  local copies, waits for them, and re-layouts  30.6 us (17%)
  between operations  13.7 us (7%)
  starting transfers between devices  7.01 us (4%)
  other arithmetic  6.27 us (3%)
    dot_general x16, matrix products, frame_block(): jnp.einsum('qsba,bak->qsbk', weights, jnp.sin(phase), precision=highest)  39.8 us
    dot_general x16, matrix products, frame_block(): jnp.einsum('qsba,bak->qsbk', weights, jnp.cos(phase), precision=highest)  39.3 us
    psum x1, waiting for transfers between devices, per_device(): summed = lax.psum(modes, 'atom')  21.1 us
    unnamed x20, local copies, waits for them, and re-layouts  13.1 us
    slice x16, local copies, waits for them, and re-layouts, frame_block(): wave_vectors[0]  12.9 us
    all_to_all x1, waiting for transfers between devices, swap_blocks(): blocks = lax.all_to_all(blocks, name, split_axis=0, concat_axis=0)  10 us
    all_to_all x1, starting transfers between devices, swap_blocks(): blocks = lax.all_to_all(blocks, name, split_axis=0, concat_axis=0)  6.78 us
    reduce_scatter x1, waiting for transfers between devices, correlate(): lax.psum_scatter(term + lag_sign[:, None] * nyq_here[None, :], 'atom', sc...  5.53 us
  transfers between devices with their start and end apart: 3, of which 3 were waited for; matrix products, arithmetic and copies ran while one was open for 0% of the time, Pallas kernels for 0%

profile of v1, /device:TPU:0, one launch (start us, length us, event | category | flops | bytes accessed | tf_op | source)
XLA Modules:
  0.0 183.2 jit_solution(5930904032424987819)
XLA Ops:
  7.2 1.0 copy.30
  8.2 0.9 reshape.85
  10.5 93.6 %while.12 = (s32[]{:T(128)}, f32[16,2,4,2,2,256]{5,2,3,4,1,0:T(4,128)S(1)}, s32[16,3,2,256]{3,2,0,1:T(2,128)S(1)}, s32[3,256]{1,0:T(4,128)}, f32[16,3,2,256]{3,1...) while((s32[]{:T(128)}, f32[16,2,4,2,2,256]{5,2,3,4,1,0:T(4,128)S(1)}, ...), condition=%wide.region_1.2_spmd, body=%wide.region_0.1_spmd.sunk | while | flops 29900800 | bytes 194661 | solution.py:115
  10.6 0.8 fusion.109
  11.4 2.5 %convolution_bitcast_fusion.5 = f32[1,4,2,2,256]{4,1,2,3,0:T(4,128)S(1)} fusion(s32[256]{0:T(256)S(1)} %bitcast.181, s32[2,256]{1,0:T(2,128)S(1)} %get-tuple-element.182, s32[256]{0:T(256)S(1)} %bitcast.183, s32[2,256]{1,0:T(2,128)S(1)} %get-tuple-element.184, s32[256]{0:T(256)S(1)} %bitcast.179, s32[2,256]{1,0:T(2,128)S(1)} %get-tuple-element.186, ...), kind=kOutput, calls=%fused_computation.1.clone.1 | convolution fusion | flops 14946304 | bytes 35840 | tf_op jit(solution)/shard_map/while/body/eval_jaxpr/qsba,bak->qsbk/dot_general | solution.py:28
  13.8 2.5 %convolution_bitcast_fusion.4 = f32[1,4,2,2,256]{4,1,2,3,0:T(4,128)S(1)} fusion(s32[256]{0:T(256)S(1)} %bitcast.182, s32[2,256]{1,0:T(2,128)S(1)} %get-tuple-element.182, s32[256]{0:T(256)S(1)} %bitcast.184, s32[2,256]{1,0:T(2,128)S(1)} %get-tuple-element.184, s32[256]{0:T(256)S(1)} %bitcast.180, s32[2,256]{1,0:T(2,128)S(1)} %get-tuple-element.186, ...), kind=kOutput, calls=%fused_computation.clone.1 | convolution fusion | flops 14946304 | bytes 35840 | tf_op jit(solution)/shard_map/while/body/eval_jaxpr/qsba,bak->qsbk/dot_general | solution.py:29
  16.4 0.8 fusion.109
  17.2 2.5 %convolution_bitcast_fusion.5 = f32[1,4,2,2,256]{4,1,2,3,0:T(4,128)S(1)} fusion(s32[256]{0:T(256)S(1)} %bitcast.181, s32[2,256]{1,0:T(2,128)S(1)} %get-tuple-element.182, s32[256]{0:T(256)S(1)} %bitcast.183, s32[2,256]{1,0:T(2,128)S(1)} %get-tuple-element.184, s32[256]{0:T(256)S(1)} %bitcast.179, s32[2,256]{1,0:T(2,128)S(1)} %get-tuple-element.186, ...), kind=kOutput, calls=%fused_computation.1.clone.1 | convolution fusion | flops 14946304 | bytes 35840 | tf_op jit(solution)/shard_map/while/body/eval_jaxpr/qsba,bak->qsbk/dot_general | solution.py:28
  19.7 2.5 %convolution_bitcast_fusion.4 = f32[1,4,2,2,256]{4,1,2,3,0:T(4,128)S(1)} fusion(s32[256]{0:T(256)S(1)} %bitcast.182, s32[2,256]{1,0:T(2,128)S(1)} %get-tuple-element.182, s32[256]{0:T(256)S(1)} %bitcast.184, s32[2,256]{1,0:T(2,128)S(1)} %get-tuple-element.184, s32[256]{0:T(256)S(1)} %bitcast.180, s32[2,256]{1,0:T(2,128)S(1)} %get-tuple-element.186, ...), kind=kOutput, calls=%fused_computation.clone.1 | convolution fusion | flops 14946304 | bytes 35840 | tf_op jit(solution)/shard_map/while/body/eval_jaxpr/qsba,bak->qsbk/dot_general | solution.py:29
  23.1 2.5 %convolution_bitcast_fusion.5 = f32[1,4,2,2,256]{4,1,2,3,0:T(4,128)S(1)} fusion(s32[256]{0:T(256)S(1)} %bitcast.181, s32[2,256]{1,0:T(2,128)S(1)} %get-tuple-element.182, s32[256]{0:T(256)S(1)} %bitcast.183, s32[2,256]{1,0:T(2,128)S(1)} %get-tuple-element.184, s32[256]{0:T(256)S(1)} %bitcast.179, s32[2,256]{1,0:T(2,128)S(1)} %get-tuple-element.186, ...), kind=kOutput, calls=%fused_computation.1.clone.1 | convolution fusion | flops 14946304 | bytes 35840 | tf_op jit(solution)/shard_map/while/body/eval_jaxpr/qsba,bak->qsbk/dot_general | solution.py:28
  25.5 2.5 %convolution_bitcast_fusion.4 = f32[1,4,2,2,256]{4,1,2,3,0:T(4,128)S(1)} fusion(s32[256]{0:T(256)S(1)} %bitcast.182, s32[2,256]{1,0:T(2,128)S(1)} %get-tuple-element.182, s32[256]{0:T(256)S(1)} %bitcast.184, s32[2,256]{1,0:T(2,128)S(1)} %get-tuple-element.184, s32[256]{0:T(256)S(1)} %bitcast.180, s32[2,256]{1,0:T(2,128)S(1)} %get-tuple-element.186, ...), kind=kOutput, calls=%fused_computation.clone.1 | convolution fusion | flops 14946304 | bytes 35840 | tf_op jit(solution)/shard_map/while/body/eval_jaxpr/qsba,bak->qsbk/dot_general | solution.py:29
  28.1 0.8 fusion.109
  28.9 2.5 %convolution_bitcast_fusion.5 = f32[1,4,2,2,256]{4,1,2,3,0:T(4,128)S(1)} fusion(s32[256]{0:T(256)S(1)} %bitcast.181, s32[2,256]{1,0:T(2,128)S(1)} %get-tuple-element.182, s32[256]{0:T(256)S(1)} %bitcast.183, s32[2,256]{1,0:T(2,128)S(1)} %get-tuple-element.184, s32[256]{0:T(256)S(1)} %bitcast.179, s32[2,256]{1,0:T(2,128)S(1)} %get-tuple-element.186, ...), kind=kOutput, calls=%fused_computation.1.clone.1 | convolution fusion | flops 14946304 | bytes 35840 | tf_op jit(solution)/shard_map/while/body/eval_jaxpr/qsba,bak->qsbk/dot_general | solution.py:28
  31.4 2.5 %convolution_bitcast_fusion.4 = f32[1,4,2,2,256]{4,1,2,3,0:T(4,128)S(1)} fusion(s32[256]{0:T(256)S(1)} %bitcast.182, s32[2,256]{1,0:T(2,128)S(1)} %get-tuple-element.182, s32[256]{0:T(256)S(1)} %bitcast.184, s32[2,256]{1,0:T(2,128)S(1)} %get-tuple-element.184, s32[256]{0:T(256)S(1)} %bitcast.180, s32[2,256]{1,0:T(2,128)S(1)} %get-tuple-element.186, ...), kind=kOutput, calls=%fused_computation.clone.1 | convolution fusion | flops 14946304 | bytes 35840 | tf_op jit(solution)/shard_map/while/body/eval_jaxpr/qsba,bak->qsbk/dot_general | solution.py:29
  34.0 0.8 fusion.109
  34.8 2.5 %convolution_bitcast_fusion.5 = f32[1,4,2,2,256]{4,1,2,3,0:T(4,128)S(1)} fusion(s32[256]{0:T(256)S(1)} %bitcast.181, s32[2,256]{1,0:T(2,128)S(1)} %get-tuple-element.182, s32[256]{0:T(256)S(1)} %bitcast.183, s32[2,256]{1,0:T(2,128)S(1)} %get-tuple-element.184, s32[256]{0:T(256)S(1)} %bitcast.179, s32[2,256]{1,0:T(2,128)S(1)} %get-tuple-element.186, ...), kind=kOutput, calls=%fused_computation.1.clone.1 | convolution fusion | flops 14946304 | bytes 35840 | tf_op jit(solution)/shard_map/while/body/eval_jaxpr/qsba,bak->qsbk/dot_general | solution.py:28
  37.2 2.5 %convolution_bitcast_fusion.4 = f32[1,4,2,2,256]{4,1,2,3,0:T(4,128)S(1)} fusion(s32[256]{0:T(256)S(1)} %bitcast.182, s32[2,256]{1,0:T(2,128)S(1)} %get-tuple-element.182, s32[256]{0:T(256)S(1)} %bitcast.184, s32[2,256]{1,0:T(2,128)S(1)} %get-tuple-element.184, s32[256]{0:T(256)S(1)} %bitcast.180, s32[2,256]{1,0:T(2,128)S(1)} %get-tuple-element.186, ...), kind=kOutput, calls=%fused_computation.clone.1 | convolution fusion | flops 14946304 | bytes 35840 | tf_op jit(solution)/shard_map/while/body/eval_jaxpr/qsba,bak->qsbk/dot_general | solution.py:29
  39.8 0.8 fusion.109
  40.7 2.5 %convolution_bitcast_fusion.5 = f32[1,4,2,2,256]{4,1,2,3,0:T(4,128)S(1)} fusion(s32[256]{0:T(256)S(1)} %bitcast.181, s32[2,256]{1,0:T(2,128)S(1)} %get-tuple-element.182, s32[256]{0:T(256)S(1)} %bitcast.183, s32[2,256]{1,0:T(2,128)S(1)} %get-tuple-element.184, s32[256]{0:T(256)S(1)} %bitcast.179, s32[2,256]{1,0:T(2,128)S(1)} %get-tuple-element.186, ...), kind=kOutput, calls=%fused_computation.1.clone.1 | convolution fusion | flops 14946304 | bytes 35840 | tf_op jit(solution)/shard_map/while/body/eval_jaxpr/qsba,bak->qsbk/dot_general | solution.py:28
  43.1 2.5 %convolution_bitcast_fusion.4 = f32[1,4,2,2,256]{4,1,2,3,0:T(4,128)S(1)} fusion(s32[256]{0:T(256)S(1)} %bitcast.182, s32[2,256]{1,0:T(2,128)S(1)} %get-tuple-element.182, s32[256]{0:T(256)S(1)} %bitcast.184, s32[2,256]{1,0:T(2,128)S(1)} %get-tuple-element.184, s32[256]{0:T(256)S(1)} %bitcast.180, s32[2,256]{1,0:T(2,128)S(1)} %get-tuple-element.186, ...), kind=kOutput, calls=%fused_computation.clone.1 | convolution fusion | flops 14946304 | bytes 35840 | tf_op jit(solution)/shard_map/while/body/eval_jaxpr/qsba,bak->qsbk/dot_general | solution.py:29
  45.7 0.8 fusion.109
  46.5 2.5 %convolution_bitcast_fusion.5 = f32[1,4,2,2,256]{4,1,2,3,0:T(4,128)S(1)} fusion(s32[256]{0:T(256)S(1)} %bitcast.181, s32[2,256]{1,0:T(2,128)S(1)} %get-tuple-element.182, s32[256]{0:T(256)S(1)} %bitcast.183, s32[2,256]{1,0:T(2,128)S(1)} %get-tuple-element.184, s32[256]{0:T(256)S(1)} %bitcast.179, s32[2,256]{1,0:T(2,128)S(1)} %get-tuple-element.186, ...), kind=kOutput, calls=%fused_computation.1.clone.1 | convolution fusion | flops 14946304 | bytes 35840 | tf_op jit(solution)/shard_map/while/body/eval_jaxpr/qsba,bak->qsbk/dot_general | solution.py:28
  49.0 2.5 %convolution_bitcast_fusion.4 = f32[1,4,2,2,256]{4,1,2,3,0:T(4,128)S(1)} fusion(s32[256]{0:T(256)S(1)} %bitcast.182, s32[2,256]{1,0:T(2,128)S(1)} %get-tuple-element.182, s32[256]{0:T(256)S(1)} %bitcast.184, s32[2,256]{1,0:T(2,128)S(1)} %get-tuple-element.184, s32[256]{0:T(256)S(1)} %bitcast.180, s32[2,256]{1,0:T(2,128)S(1)} %get-tuple-element.186, ...), kind=kOutput, calls=%fused_computation.clone.1 | convolution fusion | flops 14946304 | bytes 35840 | tf_op jit(solution)/shard_map/while/body/eval_jaxpr/qsba,bak->qsbk/dot_general | solution.py:29
  51.6 0.8 fusion.109
  52.4 2.5 %convolution_bitcast_fusion.5 = f32[1,4,2,2,256]{4,1,2,3,0:T(4,128)S(1)} fusion(s32[256]{0:T(256)S(1)} %bitcast.181, s32[2,256]{1,0:T(2,128)S(1)} %get-tuple-element.182, s32[256]{0:T(256)S(1)} %bitcast.183, s32[2,256]{1,0:T(2,128)S(1)} %get-tuple-element.184, s32[256]{0:T(256)S(1)} %bitcast.179, s32[2,256]{1,0:T(2,128)S(1)} %get-tuple-element.186, ...), kind=kOutput, calls=%fused_computation.1.clone.1 | convolution fusion | flops 14946304 | bytes 35840 | tf_op jit(solution)/shard_map/while/body/eval_jaxpr/qsba,bak->qsbk/dot_general | solution.py:28
  54.8 2.5 %convolution_bitcast_fusion.4 = f32[1,4,2,2,256]{4,1,2,3,0:T(4,128)S(1)} fusion(s32[256]{0:T(256)S(1)} %bitcast.182, s32[2,256]{1,0:T(2,128)S(1)} %get-tuple-element.182, s32[256]{0:T(256)S(1)} %bitcast.184, s32[2,256]{1,0:T(2,128)S(1)} %get-tuple-element.184, s32[256]{0:T(256)S(1)} %bitcast.180, s32[2,256]{1,0:T(2,128)S(1)} %get-tuple-element.186, ...), kind=kOutput, calls=%fused_computation.clone.1 | convolution fusion | flops 14946304 | bytes 35840 | tf_op jit(solution)/shard_map/while/body/eval_jaxpr/qsba,bak->qsbk/dot_general | solution.py:29
  58.2 2.5 %convolution_bitcast_fusion.5 = f32[1,4,2,2,256]{4,1,2,3,0:T(4,128)S(1)} fusion(s32[256]{0:T(256)S(1)} %bitcast.181, s32[2,256]{1,0:T(2,128)S(1)} %get-tuple-element.182, s32[256]{0:T(256)S(1)} %bitcast.183, s32[2,256]{1,0:T(2,128)S(1)} %get-tuple-element.184, s32[256]{0:T(256)S(1)} %bitcast.179, s32[2,256]{1,0:T(2,128)S(1)} %get-tuple-element.186, ...), kind=kOutput, calls=%fused_computation.1.clone.1 | convolution fusion | flops 14946304 | bytes 35840 | tf_op jit(solution)/shard_map/while/body/eval_jaxpr/qsba,bak->qsbk/dot_general | solution.py:28
  60.7 2.5 %convolution_bitcast_fusion.4 = f32[1,4,2,2,256]{4,1,2,3,0:T(4,128)S(1)} fusion(s32[256]{0:T(256)S(1)} %bitcast.182, s32[2,256]{1,0:T(2,128)S(1)} %get-tuple-element.182, s32[256]{0:T(256)S(1)} %bitcast.184, s32[2,256]{1,0:T(2,128)S(1)} %get-tuple-element.184, s32[256]{0:T(256)S(1)} %bitcast.180, s32[2,256]{1,0:T(2,128)S(1)} %get-tuple-element.186, ...), kind=kOutput, calls=%fused_computation.clone.1 | convolution fusion | flops 14946304 | bytes 35840 | tf_op jit(solution)/shard_map/while/body/eval_jaxpr/qsba,bak->qsbk/dot_general | solution.py:29
  64.1 2.5 %convolution_bitcast_fusion.5 = f32[1,4,2,2,256]{4,1,2,3,0:T(4,128)S(1)} fusion(s32[256]{0:T(256)S(1)} %bitcast.181, s32[2,256]{1,0:T(2,128)S(1)} %get-tuple-element.182, s32[256]{0:T(256)S(1)} %bitcast.183, s32[2,256]{1,0:T(2,128)S(1)} %get-tuple-element.184, s32[256]{0:T(256)S(1)} %bitcast.179, s32[2,256]{1,0:T(2,128)S(1)} %get-tuple-element.186, ...), kind=kOutput, calls=%fused_computation.1.clone.1 | convolution fusion | flops 14946304 | bytes 35840 | tf_op jit(solution)/shard_map/while/body/eval_jaxpr/qsba,bak->qsbk/dot_general | solution.py:28
  66.5 2.5 %convolution_bitcast_fusion.4 = f32[1,4,2,2,256]{4,1,2,3,0:T(4,128)S(1)} fusion(s32[256]{0:T(256)S(1)} %bitcast.182, s32[2,256]{1,0:T(2,128)S(1)} %get-tuple-element.182, s32[256]{0:T(256)S(1)} %bitcast.184, s32[2,256]{1,0:T(2,128)S(1)} %get-tuple-element.184, s32[256]{0:T(256)S(1)} %bitcast.180, s32[2,256]{1,0:T(2,128)S(1)} %get-tuple-element.186, ...), kind=kOutput, calls=%fused_computation.clone.1 | convolution fusion | flops 14946304 | bytes 35840 | tf_op jit(solution)/shard_map/while/body/eval_jaxpr/qsba,bak->qsbk/dot_general | solution.py:29
  69.9 2.5 %convolution_bitcast_fusion.5 = f32[1,4,2,2,256]{4,1,2,3,0:T(4,128)S(1)} fusion(s32[256]{0:T(256)S(1)} %bitcast.181, s32[2,256]{1,0:T(2,128)S(1)} %get-tuple-element.182, s32[256]{0:T(256)S(1)} %bitcast.183, s32[2,256]{1,0:T(2,128)S(1)} %get-tuple-element.184, s32[256]{0:T(256)S(1)} %bitcast.179, s32[2,256]{1,0:T(2,128)S(1)} %get-tuple-element.186, ...), kind=kOutput, calls=%fused_computation.1.clone.1 | convolution fusion | flops 14946304 | bytes 35840 | tf_op jit(solution)/shard_map/while/body/eval_jaxpr/qsba,bak->qsbk/dot_general | solution.py:28
  72.4 2.5 %convolution_bitcast_fusion.4 = f32[1,4,2,2,256]{4,1,2,3,0:T(4,128)S(1)} fusion(s32[256]{0:T(256)S(1)} %bitcast.182, s32[2,256]{1,0:T(2,128)S(1)} %get-tuple-element.182, s32[256]{0:T(256)S(1)} %bitcast.184, s32[2,256]{1,0:T(2,128)S(1)} %get-tuple-element.184, s32[256]{0:T(256)S(1)} %bitcast.180, s32[2,256]{1,0:T(2,128)S(1)} %get-tuple-element.186, ...), kind=kOutput, calls=%fused_computation.clone.1 | convolution fusion | flops 14946304 | bytes 35840 | tf_op jit(solution)/shard_map/while/body/eval_jaxpr/qsba,bak->qsbk/dot_general | solution.py:29
  75.8 2.5 %convolution_bitcast_fusion.5 = f32[1,4,2,2,256]{4,1,2,3,0:T(4,128)S(1)} fusion(s32[256]{0:T(256)S(1)} %bitcast.181, s32[2,256]{1,0:T(2,128)S(1)} %get-tuple-element.182, s32[256]{0:T(256)S(1)} %bitcast.183, s32[2,256]{1,0:T(2,128)S(1)} %get-tuple-element.184, s32[256]{0:T(256)S(1)} %bitcast.179, s32[2,256]{1,0:T(2,128)S(1)} %get-tuple-element.186, ...), kind=kOutput, calls=%fused_computation.1.clone.1 | convolution fusion | flops 14946304 | bytes 35840 | tf_op jit(solution)/shard_map/while/body/eval_jaxpr/qsba,bak->qsbk/dot_general | solution.py:28
  78.2 2.5 %convolution_bitcast_fusion.4 = f32[1,4,2,2,256]{4,1,2,3,0:T(4,128)S(1)} fusion(s32[256]{0:T(256)S(1)} %bitcast.182, s32[2,256]{1,0:T(2,128)S(1)} %get-tuple-element.182, s32[256]{0:T(256)S(1)} %bitcast.184, s32[2,256]{1,0:T(2,128)S(1)} %get-tuple-element.184, s32[256]{0:T(256)S(1)} %bitcast.180, s32[2,256]{1,0:T(2,128)S(1)} %get-tuple-element.186, ...), kind=kOutput, calls=%fused_computation.clone.1 | convolution fusion | flops 14946304 | bytes 35840 | tf_op jit(solution)/shard_map/while/body/eval_jaxpr/qsba,bak->qsbk/dot_general | solution.py:29
  81.6 2.5 %convolution_bitcast_fusion.5 = f32[1,4,2,2,256]{4,1,2,3,0:T(4,128)S(1)} fusion(s32[256]{0:T(256)S(1)} %bitcast.181, s32[2,256]{1,0:T(2,128)S(1)} %get-tuple-element.182, s32[256]{0:T(256)S(1)} %bitcast.183, s32[2,256]{1,0:T(2,128)S(1)} %get-tuple-element.184, s32[256]{0:T(256)S(1)} %bitcast.179, s32[2,256]{1,0:T(2,128)S(1)} %get-tuple-element.186, ...), kind=kOutput, calls=%fused_computation.1.clone.1 | convolution fusion | flops 14946304 | bytes 35840 | tf_op jit(solution)/shard_map/while/body/eval_jaxpr/qsba,bak->qsbk/dot_general | solution.py:28
  84.1 2.5 %convolution_bitcast_fusion.4 = f32[1,4,2,2,256]{4,1,2,3,0:T(4,128)S(1)} fusion(s32[256]{0:T(256)S(1)} %bitcast.182, s32[2,256]{1,0:T(2,128)S(1)} %get-tuple-element.182, s32[256]{0:T(256)S(1)} %bitcast.184, s32[2,256]{1,0:T(2,128)S(1)} %get-tuple-element.184, s32[256]{0:T(256)S(1)} %bitcast.180, s32[2,256]{1,0:T(2,128)S(1)} %get-tuple-element.186, ...), kind=kOutput, calls=%fused_computation.clone.1 | convolution fusion | flops 14946304 | bytes 35840 | tf_op jit(solution)/shard_map/while/body/eval_jaxpr/qsba,bak->qsbk/dot_general | solution.py:29
  87.5 2.5 %convolution_bitcast_fusion.5 = f32[1,4,2,2,256]{4,1,2,3,0:T(4,128)S(1)} fusion(s32[256]{0:T(256)S(1)} %bitcast.181, s32[2,256]{1,0:T(2,128)S(1)} %get-tuple-element.182, s32[256]{0:T(256)S(1)} %bitcast.183, s32[2,256]{1,0:T(2,128)S(1)} %get-tuple-element.184, s32[256]{0:T(256)S(1)} %bitcast.179, s32[2,256]{1,0:T(2,128)S(1)} %get-tuple-element.186, ...), kind=kOutput, calls=%fused_computation.1.clone.1 | convolution fusion | flops 14946304 | bytes 35840 | tf_op jit(solution)/shard_map/while/body/eval_jaxpr/qsba,bak->qsbk/dot_general | solution.py:28
  89.9 2.5 %convolution_bitcast_fusion.4 = f32[1,4,2,2,256]{4,1,2,3,0:T(4,128)S(1)} fusion(s32[256]{0:T(256)S(1)} %bitcast.182, s32[2,256]{1,0:T(2,128)S(1)} %get-tuple-element.182, s32[256]{0:T(256)S(1)} %bitcast.184, s32[2,256]{1,0:T(2,128)S(1)} %get-tuple-element.184, s32[256]{0:T(256)S(1)} %bitcast.180, s32[2,256]{1,0:T(2,128)S(1)} %get-tuple-element.186, ...), kind=kOutput, calls=%fused_computation.clone.1 | convolution fusion | flops 14946304 | bytes 35840 | tf_op jit(solution)/shard_map/while/body/eval_jaxpr/qsba,bak->qsbk/dot_general | solution.py:29
  93.3 2.5 %convolution_bitcast_fusion.5 = f32[1,4,2,2,256]{4,1,2,3,0:T(4,128)S(1)} fusion(s32[256]{0:T(256)S(1)} %bitcast.181, s32[2,256]{1,0:T(2,128)S(1)} %get-tuple-element.182, s32[256]{0:T(256)S(1)} %bitcast.183, s32[2,256]{1,0:T(2,128)S(1)} %get-tuple-element.184, s32[256]{0:T(256)S(1)} %bitcast.179, s32[2,256]{1,0:T(2,128)S(1)} %get-tuple-element.186, ...), kind=kOutput, calls=%fused_computation.1.clone.1 | convolution fusion | flops 14946304 | bytes 35840 | tf_op jit(solution)/shard_map/while/body/eval_jaxpr/qsba,bak->qsbk/dot_general | solution.py:28
  95.8 2.5 %convolution_bitcast_fusion.4 = f32[1,4,2,2,256]{4,1,2,3,0:T(4,128)S(1)} fusion(s32[256]{0:T(256)S(1)} %bitcast.182, s32[2,256]{1,0:T(2,128)S(1)} %get-tuple-element.182, s32[256]{0:T(256)S(1)} %bitcast.184, s32[2,256]{1,0:T(2,128)S(1)} %get-tuple-element.184, s32[256]{0:T(256)S(1)} %bitcast.180, s32[2,256]{1,0:T(2,128)S(1)} %get-tuple-element.186, ...), kind=kOutput, calls=%fused_computation.clone.1 | convolution fusion | flops 14946304 | bytes 35840 | tf_op jit(solution)/shard_map/while/body/eval_jaxpr/qsba,bak->qsbk/dot_general | solution.py:29
  99.2 2.5 %convolution_bitcast_fusion.5 = f32[1,4,2,2,256]{4,1,2,3,0:T(4,128)S(1)} fusion(s32[256]{0:T(256)S(1)} %bitcast.181, s32[2,256]{1,0:T(2,128)S(1)} %get-tuple-element.182, s32[256]{0:T(256)S(1)} %bitcast.183, s32[2,256]{1,0:T(2,128)S(1)} %get-tuple-element.184, s32[256]{0:T(256)S(1)} %bitcast.179, s32[2,256]{1,0:T(2,128)S(1)} %get-tuple-element.186, ...), kind=kOutput, calls=%fused_computation.1.clone.1 | convolution fusion | flops 14946304 | bytes 35840 | tf_op jit(solution)/shard_map/while/body/eval_jaxpr/qsba,bak->qsbk/dot_general | solution.py:28
  101.7 2.5 %convolution_bitcast_fusion.4 = f32[1,4,2,2,256]{4,1,2,3,0:T(4,128)S(1)} fusion(s32[256]{0:T(256)S(1)} %bitcast.182, s32[2,256]{1,0:T(2,128)S(1)} %get-tuple-element.182, s32[256]{0:T(256)S(1)} %bitcast.184, s32[2,256]{1,0:T(2,128)S(1)} %get-tuple-element.184, s32[256]{0:T(256)S(1)} %bitcast.180, s32[2,256]{1,0:T(2,128)S(1)} %get-tuple-element.186, ...), kind=kOutput, calls=%fused_computation.clone.1 | convolution fusion | flops 14946304 | bytes 35840 | tf_op jit(solution)/shard_map/while/body/eval_jaxpr/qsba,bak->qsbk/dot_general | solution.py:29
  104.6 0.8 pad_maximum_fusion
  105.4 21.1 %all-reduce.3.cloned.1.call-done = f32[2,2,2,32,256]{4,2,3,1,0:T(2,128)} async-done(((f32[2,2,2,32,256]{4,2,3,1,0:T(2,128)}), f32[2,2,2,32,256]{4,2,3,1,0:T(2,128)}) %all-reduce.3.cloned.1.call-update) | async-done | bytes 262160 | tf_op jit(solution)/shard_map/psum | solution.py:128
  126.6 1.0 fusion.67
  127.6 1.2 fusion.66
  128.7 1.2 fusion.65
  129.9 1.2 fusion.64
  131.0 1.2 fusion.63
  132.2 1.2 fusion.62
  133.4 1.2 fusion.61
  134.5 1.2 fusion.60
  137.6 0.9 copy.33
  138.5 1.1 reshape.97
  139.7 6.8 %all-to-all-start = ((f32[16,1,4096]{2,1,0:T(1,128)}), f32[16,1,4096]{2,1,0:T(1,128)S(1)}, u32[]{:S(2)}, u32[]{:S(2)}) async-start(f32[16,1,4096]{2,1,0:T(1,128)} %reshape.97), calls=%async_computation | async-start | bytes 524288 | tf_op jit(solution)/shard_map/all_to_all | solution.py:14
  146.8 10.0 %all-to-all-done = f32[16,1,4096]{2,1,0:T(1,128)S(1)} async-done(((f32[16,1,4096]{2,1,0:T(1,128)}), f32[16,1,4096]{2,1,0:T(1,128)S(1)}, u32[]{:S(2)}, u32[]{:S(2)}) %all-to-all-start) | async-done | bytes 262176 | tf_op jit(solution)/shard_map/all_to_all | solution.py:14
  157.3 1.3 reduce
  160.1 2.3 %fusion.28 = f32[2,2,2,16,256]{4,3,2,1,0:T(8,128)S(1)} fusion(f32[2,2,2,512,16]{3,4,2,1,0:T(8,128)S(1)} %reshape.89, s32[256]{0:T(256)S(1)} %iota_add_fusion), kind=kOutput, calls=%fused_computation.41 | convolution fusion | flops 203161600 | bytes 394240 | tf_op jit(solution)/shard_map/dot_general | solution.py:73
  162.4 2.3 %fusion.30 = f32[2,2,2,16,256]{4,3,2,1,0:T(8,128)S(1)} fusion(f32[2,2,2,512,16]{3,4,2,1,0:T(8,128)S(1)} %reshape.89, s32[256]{0:T(256)S(1)} %iota_add_fusion), kind=kOutput, calls=%fused_computation.43 | convolution fusion | flops 203161600 | bytes 394240 | tf_op jit(solution)/shard_map/dot_general | solution.py:70
  164.8 1.0 fusion.40
  166.1 1.3 fusion.47
  167.4 2.0 %fusion.24 = f32[256,96]{0,1:T(8,128)} fusion(f32[256,96]{0,1:T(8,128)S(1)} %fusion.47, f32[96,256]{1,0:T(8,128)S(1)} %get-tuple-element.134, s32[256]{0:T(256)S(1)} %iota_add_fusion, f32[96]{0:T(128)S(1)} %mul.346, f32[256]{0:T(256)S(1)} %compare_select_fusion), kind=kOutput, calls=%fused_computation.34 | convolution fusion | flops 76488704 | bytes 297344 | tf_op jit(solution)/shard_map/dot_general | solution.py:91
  169.5 5.5 %reduce-scatter.2.cloned.1.call-done = f32[128,96]{0,1:T(8,128)} async-done(((f32[256,96]{0,1:T(8,128)}), f32[128,96]{0,1:T(8,128)}) %reduce-scatter.2.cloned.1.call-update) | async-done | bytes 49168 | tf_op jit(solution)/shard_map/reduce_scatter | solution.py:95
  175.0 1.4 multiply_divide_fusion
  (129 shorter events, 14.9 us)
Async XLA Ops:
  6.5 120.0 %all-reduce.3.cloned.1.call-start = ((), (), s32[]{:S(2)}) async-start(), calls=%async_computation.2 | async-start | bytes 524288 | tf_op jit(solution)/shard_map/psum | solution.py:128
  126.6 9.1 %copy-start = (f32[2,2,2,32,256]{4,2,3,1,0:T(2,128)S(1)}, f32[2,2,2,32,256]{4,2,3,1,0:T(2,128)}, u32[]{:S(2)}) copy-start(f32[2,2,2,32,256]{4,2,3,1,0:T(2,128)} %all-reduce.3.cloned.1.call-done) | copy-start | bytes 786436
  139.7 17.1 %all-to-all-start = ((f32[16,1,4096]{2,1,0:T(1,128)}), f32[16,1,4096]{2,1,0:T(1,128)S(1)}, u32[]{:S(2)}, u32[]{:S(2)}) async-start(f32[16,1,4096]{2,1,0:T(1,128)} %reshape.97), calls=%async_computation | async-start | bytes 524288 | tf_op jit(solution)/shard_map/all_to_all | solution.py:14
  146.5 28.5 %reduce-scatter.2.cloned.1.call-start = ((), (), s32[]{:S(2)}) async-start(), calls=%async_computation.3 | async-start | bytes 147456 | tf_op jit(solution)/shard_map/reduce_scatter | solution.py:95
Sparse Core Ops, SparseCore 0:
  105.6 20.9 all-reduce.2
  169.6 5.3 reduce-scatter.1
